TPU v7x, 32 devices: a whole 2x2x4 slice. The times are simulated.
32 devices in a mesh: grp: 2 (over x), row: 16 (over z, y, core).
Axes of the slice: x: 2, y: 2, z: 4, core: 2. Of those that a mesh axis runs over, the one named last changes fastest.
Arguments:
- excitations: bfloat16 [32, 8192, 128], P('grp', 'row'), parts along dimension 0, may hold values from -0.005859375 to 0.005859375
- valence_orb: bfloat16 [2048, 128], P(('grp', 'row')), parts along dimension 0, may hold values from -6 to 6
- conduction_orb: bfloat16 [2048, 8192], P(('grp', 'row')), parts along dimension 0, may hold values from -6 to 6
- screened: bfloat16 [2048, 1024], P(('grp', 'row')), parts along dimension 0, may hold values from -0.005859375 to 0.005859375
Outputs:
- action: bfloat16 [32, 8192, 128], P('grp', 'row'), parts along dimension 0
There are 2 independent parts, one for each index of `grp`. A program takes and returns all parts, laid end to end along the dimension named above; each array names one. Nothing has to cross between parts.
All inputs are finite; a program needn't handle non-finite values.
Results may differ from a plain program's by a relative error of at most 0.0064.
Values may be sent and summed in bfloat16 or wider, within the bound.
A program may use at most 64 MiB of HBM per device.

v0:
```python
import math

import jax
import jax.numpy as jnp
from jax import lax
from jax.sharding import PartitionSpec as P


def over_blocks(total_rows, step_fn, initial):
    span_size = math.gcd(total_rows, 2048)
    block_count = total_rows // span_size
    if block_count == 1:
        return step_fn(initial, 0, span_size)
    return lax.fori_loop(
        0, block_count, lambda index, carry: step_fn(carry, index * span_size, span_size), initial
    )


def density_rows(flat_exc, batch, valence_rows, cond_rows):
    total_rows = valence_rows.shape[0]
    cond_local = cond_rows.shape[1]
    initial = jnp.zeros((batch, total_rows), jnp.float32)

    def step_fn(carry, offset, span_size):
        val_block = lax.dynamic_slice_in_dim(valence_rows, offset, span_size, 0)
        cond_block = lax.dynamic_slice_in_dim(cond_rows, offset, span_size, 0)
        mixed = lax.dot_general(
            flat_exc, val_block, (((1,), (1,)), ((), ())), preferred_element_type=jnp.float32
        )
        mixed = mixed.reshape(batch, cond_local, span_size)
        summed = jnp.sum(mixed * cond_block.T.astype(jnp.float32)[None], axis=1)
        return lax.dynamic_update_slice_in_dim(carry, summed, offset, 1)

    return over_blocks(total_rows, step_fn, initial)


def projection(carry, valence_rows, cond_rows, field_cols):
    total_rows = valence_rows.shape[0]
    batch = field_cols.shape[0]
    cond_local = cond_rows.shape[1]

    def step_fn(inner, offset, span_size):
        val_block = lax.dynamic_slice_in_dim(valence_rows, offset, span_size, 0)
        cond_block = lax.dynamic_slice_in_dim(cond_rows, offset, span_size, 0)
        field_block = lax.dynamic_slice_in_dim(field_cols, offset, span_size, 1)
        pair = (
            cond_block.T.astype(jnp.float32)[None] * field_block.astype(jnp.float32)[:, None, :]
        ).astype(jnp.bfloat16)
        pair = pair.reshape(batch * cond_local, span_size)
        return inner + jnp.dot(pair, val_block, preferred_element_type=jnp.float32)

    return over_blocks(total_rows, step_fn, carry)


def body(excitations, valence_orb, conduction_orb, screened):
    batch, cond_local, valence = excitations.shape
    flat_exc = excitations.reshape(batch * cond_local, valence)
    valence_whole = lax.all_gather(valence_orb, "row", axis=0, tiled=True)
    cond_rows = lax.all_to_all(conduction_orb, "row", split_axis=1, concat_axis=0, tiled=True)
    partial_density = density_rows(flat_exc, batch, valence_whole, cond_rows)
    density_whole = lax.psum(partial_density, "row").astype(jnp.bfloat16)
    field_mine = lax.dot_general(
        density_whole, screened, (((1,), (1,)), ((), ())), preferred_element_type=jnp.float32
    ).astype(jnp.bfloat16)
    initial = jnp.zeros((batch * cond_local, valence), jnp.float32)
    summed = projection(
        initial, valence_whole, cond_rows, lax.all_gather(field_mine, "row", axis=1, tiled=True)
    )
    return summed.reshape(batch, cond_local, valence).astype(jnp.bfloat16)


def solution(mesh):
    in_specs = (
        P("grp", "row", None),
        P(("grp", "row"), None),
        P(("grp", "row"), None),
        P(("grp", "row"), None),
    )
    out_specs = P("grp", "row", None)
    return jax.shard_map(body, mesh=mesh, in_specs=in_specs, out_specs=out_specs, check_vma=False)
```

profile of v0, /device:TPU:0, one launch (start us, length us, event | category | flops | bytes accessed | tf_op | source)
XLA Modules:
  0.0 141.2 jit_solution(12085013585132656083)
XLA Ops:
  0.0 0.0 copy-start
  0.0 0.0 copy-start.2
  0.0 2.5 %copy.15 = bf16[8,16,8,512]{3,2,0,1:T(8,128)(2,1)} copy(bf16[8,16,8,512]{3,2,1,0:T(8,128)(2,1)} %bitcast.26) | data formatting | bytes 2097152 | tf_op jit(solution)/shard_map/all_to_all | solution.py:59
  2.5 7.4 %all-to-all-start = ((bf16[64,16,512]{2,0,1:T(8,128)(2,1)}), bf16[64,16,512]{2,0,1:T(8,128)(2,1)S(1)}, u32[]{:S(2)}, u32[]{:S(2)}) async-start(bf16[64,16,512]{2,0,1:T(8,128)(2,1)} %bitcast.25), calls=%async_computation | async-start | bytes 2097152 | tf_op jit(solution)/shard_map/all_to_all | solution.py:59
  9.9 0.0 copy-done.2
  9.9 34.5 %all_gather.6 = bf16[1024,128]{1,0:T(8,128)(2,1)S(1)} all-gather(bf16[64,128]{1,0:T(8,128)(2,1)S(1)} %copy-done.2), channel_id=1, replica_groups=mesh['grp'=2,'row'=16] {'row'}, dimensions={0}, use_global_device_ids=true | all-gather | bytes 278528 | tf_op jit(solution)/shard_map/all_gather | solution.py:58
  44.4 0.0 all-to-all-done
  44.4 1.6 %convert_element_type.41 = f32[64,16,512]{2,0,1:T(8,128)} convert(bf16[64,16,512]{2,0,1:T(8,128)(2,1)S(1)} %all-to-all-done) | non-fusion elementwise | flops 524288 | bytes 3145728 | tf_op jit(solution)/shard_map/convert_element_type | solution.py:47
  46.0 2.9 %copy.11 = f32[512,1024]{1,0:T(8,128)} copy(f32[512,1024]{0,1:T(8,128)} %bitcast.24) | data formatting | bytes 4194304 | tf_op jit(solution)/shard_map/convert_element_type | solution.py:47
  48.9 0.0 copy-done
  48.9 0.0 copy-start.1
  48.9 6.0 %multiply_reduce_fusion = f32[16,1024]{1,0:T(8,128)S(1)} fusion(f32[512,1024]{1,0:T(8,128)} %copy.11, bf16[16,512,128]{2,1,0:T(8,128)(2,1)S(1)} %copy-done, bf16[1024,128]{1,0:T(8,128)(2,1)S(1)} %all_gather.6), kind=kOutput, calls=%fused_computation.1 | convolution fusion | flops 2164244480 | bytes 4521984 | tf_op jit(solution)/shard_map/dot_general | solution.py:27
  54.9 61.8 %psum.7 = bf16[16,1024]{1,0:T(8,128)(2,1)S(1)} all-reduce(f32[16,1024]{1,0:T(8,128)S(1)} %multiply_reduce_fusion), channel_id=1, replica_groups=mesh['grp'=2,'row'=16] {'row'}, use_global_device_ids=true, to_apply=%region_1.0 | all-reduce | flops 16384 | bytes 98304 | tf_op jit(solution)/shard_map/psum | solution.py:61
  116.7 0.0 copy-done.1
  116.7 0.1 fusion.4
  116.9 17.3 %all-gather = bf16[16,64,16]{1,2,0:T(8,128)(2,1)S(1)} all-gather(bf16[1,64,16]{1,2,0:T(8,128)(2,1)S(1)} %fusion.4), channel_id=1, replica_groups=mesh['grp'=2,'row'=16] {'row'}, dimensions={0}, use_global_device_ids=true | all-gather | bytes 34816 | tf_op jit(solution)/shard_map/all_gather | solution.py:67
  134.2 0.1 reshape.19
  134.3 6.9 %fusion.3 = bf16[16,512,128]{2,1,0:T(8,128)(2,1)} fusion(f32[16,1024]{1,0:T(8,128)S(1)} %bitcast.27, f32[512,1024]{1,0:T(8,128)} %copy.11, bf16[1024,128]{1,0:T(8,128)(2,1)S(1)} %all_gather.6), kind=kOutput, calls=%fused_computation.5 | convolution fusion | flops 2165309440 | bytes 4521984 | tf_op jit(solution)/shard_map/dot_general | solution.py:50
  (1 shorter events, 0.0 us)
Async XLA Ops:
  0.0 48.9 %copy-start = (bf16[16,512,128]{2,1,0:T(8,128)(2,1)S(1)}, bf16[16,512,128]{2,1,0:T(8,128)(2,1)}, u32[]{:S(2)}) copy-start(bf16[16,512,128]{2,1,0:T(8,128)(2,1)} %param.4) | copy-start | bytes 6291460
  0.0 9.9 %copy-start.2 = (bf16[64,128]{1,0:T(8,128)(2,1)S(1)}, bf16[64,128]{1,0:T(8,128)(2,1)}, u32[]{:S(2)}) copy-start(bf16[64,128]{1,0:T(8,128)(2,1)} %param.5) | copy-start | bytes 49156
  2.5 41.9 %all-to-all-start = ((bf16[64,16,512]{2,0,1:T(8,128)(2,1)}), bf16[64,16,512]{2,0,1:T(8,128)(2,1)S(1)}, u32[]{:S(2)}, u32[]{:S(2)}) async-start(bf16[64,16,512]{2,0,1:T(8,128)(2,1)} %bitcast.25), calls=%async_computation | async-start | bytes 2097152 | tf_op jit(solution)/shard_map/all_to_all | solution.py:59
  48.9 67.8 %copy-start.1 = (bf16[64,1024]{1,0:T(8,128)(2,1)S(1)}, bf16[64,1024]{1,0:T(8,128)(2,1)}, u32[]{:S(2)}) copy-start(bf16[64,1024]{1,0:T(8,128)(2,1)} %param.7) | copy-start | bytes 393220
where the time goes:
time: 142 us; the launch traced here: 141 us
  blocking collectives  114 us (80%)
  matrix products  13.1 us (9%)
  starting transfers between devices  7.41 us (5%)
  local copies, waits for them, and re-layouts  5.54 us (4%)
  other arithmetic  1.6 us (1%)
    psum x1, blocking collectives, body(): density_whole = lax.psum(partial_density, 'row').astype(jnp.bfloat16)  61.8 us
    all_gather x1, blocking collectives, body(): valence_whole = lax.all_gather(valence_orb, 'row', axis=0, tiled=True)  34.5 us
    all_gather x1, blocking collectives, body(): lax.all_gather(field_mine, 'row', axis=1, tiled=True)  17.3 us
    all_to_all x1, starting transfers between devices, body(): lax.all_to_all(conduction_orb, 'row', split_axis=1, concat_axis=0, tiled=...  7.41 us
    dot_general x1, matrix products, step_fn(): return inner + jnp.dot(pair, val_block, preferred_element_type=jnp.float32)  6.93 us
    dot_general x1, matrix products, step_fn(): lax.dot_general(flat_exc, val_block, (((1,), (1,)), ((), ())), preferred_...  6.01 us
    convert_element_type x1, local copies, waits for them, and re-layouts, step_fn(): cond_block.T.astype(jnp.float32)[None]  2.94 us
  transfers between devices with their start and end apart: 1, of which 0 were waited for; matrix products, arithmetic and copies ran while one was open for 0% of the time, Pallas kernels for 0%

commit v1 on v0

--- a/solution.py
+++ b/solution.py
@@ -1,9 +1,251 @@
+import functools
 import math
 
 import jax
 import jax.numpy as jnp
 from jax import lax
+from jax.experimental import pallas as pl
+from jax.experimental.pallas import tpu as pltpu
 from jax.sharding import PartitionSpec as P
+
+MESH = pl.DeviceIdType.MESH
+NT = (((1,), (1,)), ((), ()))
+
+
+def flip(index, other, bits):
+    total = 0
+    for bit in range(bits):
+        a = (index // (1 << bit)) % 2
+        b = (other // (1 << bit)) % 2
+        total = total + (a + b - 2 * a * b) * (1 << bit)
+    return total
+
+
+def gather_kernel(
+    n, planes,
+    exc_hbm, val_ref, cond_hbm, scr_ref,
+    condt_ref, valt_ref, field_ref,
+    exc, exct, cond_all, val_all, scr_chip, part, red, dens, dens_all, fld, fld_all,
+    exc_sem, own_sem,
+    cond_send, cond_recv, scr_send, scr_recv, va_send, va_recv, vb_send, vb_recv,
+    part_send, part_recv, dens_send, dens_recv, fld_send, fld_recv,
+):
+    rows, cl = val_ref.shape[0], exc.shape[1]
+    batch = exc.shape[0]
+    half = batch // 2
+    q = n // planes
+    bits = n.bit_length() - 1
+    chips = n // 2
+    me = lax.axis_index("row")
+    my_z, my_q = me // q, me % q
+    chip, core = me // 2, me % 2
+
+    exc_copy = pltpu.make_async_copy(exc_hbm, exc, exc_sem)
+    exc_copy.start()
+    own_val = pltpu.make_async_copy(val_ref, val_all.at[my_q, my_z], own_sem.at[0])
+    own_val.start()
+    own_scr = pltpu.make_async_copy(scr_ref, scr_chip.at[core], own_sem.at[1])
+    own_scr.start()
+    pltpu.make_async_copy(
+        cond_hbm.at[:, pl.ds(pl.multiple_of(me * cl, cl), cl)], cond_all.at[me], cond_recv.at[me]
+    ).start()
+
+    barrier = pltpu.get_barrier_semaphore()
+    for k in range(1, n):
+        pl.semaphore_signal(barrier, inc=1, device_id={"row": flip(me, k, bits)}, device_id_type=MESH)
+    pl.semaphore_wait(barrier, n - 1)
+
+    def remote(src, dst, send, recv, to):
+        return pltpu.make_async_remote_copy(
+            src_ref=src, dst_ref=dst, send_sem=send, recv_sem=recv,
+            device_id={"row": to}, device_id_type=MESH,
+        )
+
+    sent = []
+    zbits, qbits = planes.bit_length() - 1, q.bit_length() - 1
+    for k in range(planes - 1, 0, -1):
+        to = flip(my_z, k, zbits) * q + my_q
+        copy = remote(val_ref, val_all.at[my_q, my_z], va_send.at[k], va_recv.at[my_z], to)
+        copy.start()
+        sent.append(copy)
+    for k in range(n - 1, 0, -1):
+        to = flip(me, k, bits)
+        copy = remote(
+            cond_hbm.at[:, pl.ds(pl.multiple_of(to * cl, cl), cl)], cond_all.at[me],
+            cond_send.at[k], cond_recv.at[me], to,
+        )
+        copy.start()
+        sent.append(copy)
+    copy = remote(scr_ref, scr_chip.at[core], scr_send, scr_recv, chip * 2 + 1 - core)
+    copy.start()
+    sent.append(copy)
+
+    exc_copy.wait()
+
+    def turn(b, carry):
+        exct[pl.ds(pl.multiple_of(b * 128, 128), 128), :] = exc[b].T
+        return carry
+
+    lax.fori_loop(0, batch, turn, 0)
+
+    own_val.wait()
+    for k in range(1, planes):
+        z = flip(my_z, k, zbits)
+        pltpu.make_async_copy(val_ref, val_all.at[my_q, z], va_recv.at[z]).wait()
+    for k in range(1, q):
+        to = my_z * q + flip(my_q, k, qbits)
+        copy = remote(val_all.at[my_q], val_all.at[my_q], vb_send.at[k], vb_recv.at[my_q], to)
+        copy.start()
+        sent.append(copy)
+    for k in range(1, q):
+        other = flip(my_q, k, qbits)
+        pltpu.make_async_copy(val_all.at[other], val_all.at[other], vb_recv.at[other]).wait()
+
+    def group(k, carry):
+        p = flip(chip, k, bits - 1)
+        z, y = p // (q // 2), p % (q // 2)
+        lanes = pl.ds(pl.multiple_of(p * 2 * rows, 2 * rows), 2 * rows)
+        for h in range(2):
+            pltpu.make_async_copy(cond_all.at[2 * p + h], cond_all.at[2 * p + h], cond_recv.at[2 * p + h]).wait()
+        block = cond_all[pl.ds(2 * p, 2)].reshape(2 * rows, cl)
+        vals = jnp.concatenate([val_all[2 * y, z], val_all[2 * y + 1, z]], axis=0)
+        valt = vals.astype(jnp.float32).T
+        valt_ref[:, lanes] = valt.astype(jnp.bfloat16)
+        mixed = lax.dot_general(exct[...], block, NT, preferred_element_type=jnp.float32)
+        summed = jnp.sum(mixed.reshape(batch, valt.shape[0], 2 * rows) * valt[None], axis=1)
+        part[k, 0] = summed[:half]
+        part[k, 1] = summed[half:]
+
+        @pl.when(k == 0)
+        def _():
+            remote(
+                part.at[k, 1 - core], red.at[me], part_send.at[k, 1 - core], part_recv.at[me],
+                2 * chip + 1 - core,
+            ).start()
+            red[me] = part[0, core]
+
+        @pl.when(k > 0)
+        def _():
+            for h in range(2):
+                remote(
+                    part.at[k, h], red.at[me], part_send.at[k, h], part_recv.at[me], 2 * p + h
+                ).start()
+
+        condt_ref[:, lanes] = block.T
+        return carry
+
+    lax.fori_loop(0, chips, group, 0)
+
+    own_scr.wait()
+    pltpu.make_async_copy(scr_chip.at[1 - core], scr_chip.at[1 - core], scr_recv).wait()
+    total = red[me]
+    for k in range(1, n):
+        other = flip(me, k, bits)
+        pltpu.make_async_copy(red.at[other], red.at[other], part_recv.at[other]).wait()
+        total = total + red[other]
+    dens[...] = total.astype(jnp.bfloat16)
+    dens_all[chip] = total.astype(jnp.bfloat16)
+    for k in range(chips - 1, 0, -1):
+        to = flip(chip, k, bits - 1)
+        copy = remote(dens, dens_all.at[chip], dens_send.at[k], dens_recv.at[chip], 2 * to + core)
+        copy.start()
+        sent.append(copy)
+    for k in range(1, chips):
+        other = flip(chip, k, bits - 1)
+        pltpu.make_async_copy(dens_all.at[other], dens_all.at[other], dens_recv.at[other]).wait()
+    whole = jnp.concatenate([dens_all[p].astype(jnp.float32) for p in range(chips)], axis=1).astype(jnp.bfloat16)
+    screened = scr_chip[...].reshape(2 * rows, scr_ref.shape[1])
+    mine = lax.dot_general(whole, screened, NT, preferred_element_type=jnp.float32).astype(jnp.bfloat16)
+    fld[...] = mine
+    fld_all[me] = mine
+    for k in range(n - 1, 0, -1):
+        copy = remote(fld, fld_all.at[me], fld_send.at[k], fld_recv.at[me], flip(me, k, bits))
+        copy.start()
+        sent.append(copy)
+    for k in range(1, n):
+        other = flip(me, k, bits)
+        pltpu.make_async_copy(fld_all.at[other], fld_all.at[other], fld_recv.at[other]).wait()
+    for p in range(chips):
+        for h in range(2):
+            field_ref[h * half:(h + 1) * half, p * 2 * rows:(p + 1) * 2 * rows] = fld_all[2 * p + h].astype(jnp.float32)
+
+    for copy in sent:
+        copy.wait_send()
+    remote(
+        part.at[0, 1 - core], red.at[me], part_send.at[0, 1 - core], part_recv.at[me], 2 * chip + 1 - core
+    ).wait_send()
+    for k in range(1, chips):
+        p = flip(chip, k, bits - 1)
+        for h in range(2):
+            remote(part.at[k, h], red.at[me], part_send.at[k, h], part_recv.at[me], 2 * p + h).wait_send()
+
+
+def project_kernel(per, condt_ref, valt_ref, field_ref, out_ref):
+    step = pl.program_id(0)
+    v = valt_ref.shape[0]
+    valt = valt_ref[...].astype(jnp.float32)
+    for j in range(0, per, 2):
+        weights = jnp.concatenate(
+            [(valt * field_ref[pl.ds(step * per + j + i, 1), :]).astype(jnp.bfloat16) for i in range(2)], axis=0
+        )
+        summed = lax.dot_general(condt_ref[...], weights, NT, preferred_element_type=jnp.float32)
+        for i in range(2):
+            out_ref[j + i] = summed[:, i * v:(i + 1) * v].astype(jnp.bfloat16)
+
+
+def fast_body(n, excitations, valence_orb, conduction_orb, screened):
+    batch, cl, v = excitations.shape
+    rows, points = screened.shape
+    planes = 4 if n % 8 == 0 else 2
+    q, chips, half = n // planes, n // 2, batch // 2
+    bf, f32 = jnp.bfloat16, jnp.float32
+    any_ = pl.BlockSpec(memory_space=pl.ANY)
+    vmem = pl.BlockSpec(memory_space=pltpu.VMEM)
+    dma = pltpu.SemaphoreType.DMA
+    condt, valt, field = pl.pallas_call(
+        functools.partial(gather_kernel, n, planes),
+        out_shape=(
+            jax.ShapeDtypeStruct((cl, points), bf),
+            jax.ShapeDtypeStruct((v, points), bf),
+            jax.ShapeDtypeStruct((batch, points), f32),
+        ),
+        in_specs=[any_, vmem, any_, vmem],
+        out_specs=(vmem, vmem, vmem),
+        scratch_shapes=[
+            pltpu.VMEM((batch, cl, v), bf),
+            pltpu.VMEM((batch * v, cl), bf),
+            pltpu.VMEM((n, rows, cl), bf),
+            pltpu.VMEM((q, planes, rows, v), bf),
+            pltpu.VMEM((2, rows, points), bf),
+            pltpu.VMEM((chips, 2, half, 2 * rows), f32),
+            pltpu.VMEM((n, half, 2 * rows), f32),
+            pltpu.VMEM((half, 2 * rows), bf),
+            pltpu.VMEM((chips, half, 2 * rows), bf),
+            pltpu.VMEM((half, 2 * rows), bf),
+            pltpu.VMEM((n, half, 2 * rows), bf),
+            dma, dma((2,)),
+            dma((n,)), dma((n,)), dma, dma, dma((planes,)), dma((planes,)), dma((q,)), dma((q,)),
+            dma((chips, 2)), dma((n,)), dma((chips,)), dma((chips,)), dma((n,)), dma((n,)),
+        ],
+        compiler_params=pltpu.CompilerParams(
+            collective_id=0, has_side_effects=True, vmem_limit_bytes=40 * 1024 * 1024
+        ),
+        name="gather_field",
+    )(excitations, valence_orb, conduction_orb, screened)
+    per = 4
+    whole = lambda i: (0, 0)
+    return pl.pallas_call(
+        functools.partial(project_kernel, per),
+        grid=(batch // per,),
+        out_shape=jax.ShapeDtypeStruct((batch, cl, v), bf),
+        in_specs=[
+            pl.BlockSpec((cl, points), whole),
+            pl.BlockSpec((v, points), whole),
+            pl.BlockSpec((batch, points), whole),
+        ],
+        out_specs=pl.BlockSpec((per, cl, v), lambda i: (i, 0, 0)),
+        name="project",
+    )(condt, valt, field)
 
 
 def over_blocks(total_rows, step_fn, initial):
@@ -52,7 +294,7 @@
     return over_blocks(total_rows, step_fn, carry)
 
 
-def body(excitations, valence_orb, conduction_orb, screened):
+def general_body(excitations, valence_orb, conduction_orb, screened):
     batch, cond_local, valence = excitations.shape
     flat_exc = excitations.reshape(batch * cond_local, valence)
     valence_whole = lax.all_gather(valence_orb, "row", axis=0, tiled=True)
@@ -69,6 +311,15 @@
     return summed.reshape(batch, cond_local, valence).astype(jnp.bfloat16)
 
 
+def body(n, excitations, valence_orb, conduction_orb, screened):
+    batch, cl, v = excitations.shape
+    rows = valence_orb.shape[0]
+    fits = n in (8, 16) and cl % 128 == 0 and v == 128 and rows == 64 and batch == 16
+    if fits:
+        return fast_body(n, excitations, valence_orb, conduction_orb, screened)
+    return general_body(excitations, valence_orb, conduction_orb, screened)
+
+
 def solution(mesh):
     in_specs = (
         P("grp", "row", None),
@@ -77,4 +328,7 @@
         P(("grp", "row"), None),
     )
     out_specs = P("grp", "row", None)
-    return jax.shard_map(body, mesh=mesh, in_specs=in_specs, out_specs=out_specs, check_vma=False)
+    return jax.shard_map(
+        functools.partial(body, mesh.shape["row"]),
+        mesh=mesh, in_specs=in_specs, out_specs=out_specs, check_vma=False,
+    )

time: 142 us -> 61.2 us (0.43)
  blocking collectives: 114 us -> 0 us
  Pallas kernels: 0 us -> 54.2 us
  matrix products: 13.1 us -> 0 us
  starting transfers between devices: 7.41 us -> 0 us
  other arithmetic: 1.6 us -> 0 us
    psum x1 -> x0, blocking collectives: 61.8 us -> none  [body(): density_whole = lax.psum(partial_density, 'row').astype(jnp.bfloat16)]
    pallas_call x0 -> x2, Pallas kernels: none -> 54.2 us  [the longest x1 49 us: fast_body(): pl.pallas_call(functools.partial(gather_kernel, n, planes), out_shape=(ja...]
    all_gather x2 -> x0, blocking collectives: 51.7 us -> none  [the longest x1 34.5 us: body(): valence_whole = lax.all_gather(valence_orb, 'row', axis=0, tiled=True)]
    dot_general x3 -> x0, matrix products: 13.1 us -> none  [the longest x1 6.93 us: step_fn(): return inner + jnp.dot(pair, val_block, preferred_element_type=jnp.float32)]
    all_to_all x1 -> x0, starting transfers between devices: 7.41 us -> none  [body(): lax.all_to_all(conduction_orb, 'row', split_axis=1, concat_axis=0, tiled=...]
    unnamed x6 -> x14, local copies, waits for them, and re-layouts: 0.01 us -> 6.71 us
    convert_element_type x3 -> x0, local copies, waits for them, and re-layouts: 3.06 us -> none  [the longest x1 2.94 us: step_fn(): cond_block.T.astype(jnp.float32)[None]]
    all_to_all x1 -> x0, local copies, waits for them, and re-layouts: 2.47 us -> none  [body(): lax.all_to_all(conduction_orb, 'row', split_axis=1, concat_axis=0, tiled=...]
  transfers between devices with their start and end apart: 1 -> 0, of which waited for: 0 -> 0; matrix products, arithmetic and copies ran while one was open for 0% -> 0% of each run, Pallas kernels for 0% -> 0%
where the time goes in v1:
time: 61.2 us; the launch traced here: 60.9 us
  Pallas kernels  54.2 us (89%)
  local copies, waits for them, and re-layouts  6.71 us (11%)
    pallas_call x1, Pallas kernels, fast_body(): pl.pallas_call(functools.partial(gather_kernel, n, planes), out_shape=(ja...  49 us
    unnamed x14, local copies, waits for them, and re-layouts  6.71 us
    pallas_call x1, Pallas kernels, fast_body(): pl.pallas_call(functools.partial(project_kernel, per), grid=(batch // per...  5.19 us

profile of v1, /device:TPU:0, one launch (start us, length us, event | category | flops | bytes accessed | tf_op | source)
XLA Modules:
  0.0 60.9 jit_solution(505949806133949044)
XLA Ops:
  0.0 0.0 copy-start
  0.0 1.6 %copy-done = bf16[16,512,128]{2,1,0:T(8,128)(2,1)S(1)} copy-done((bf16[16,512,128]{2,1,0:T(8,128)(2,1)S(1)}, bf16[16,512,128]{2,1,0:T(8,128)(2,1)}, u32[]{:S(2)}) %copy-start) | copy-done | bytes 2097176
  1.6 0.0 copy-start.1
  1.6 1.2 %copy-done.1 = bf16[64,8192]{1,0:T(8,128)(2,1)S(1)} copy-done((bf16[64,8192]{1,0:T(8,128)(2,1)S(1)}, bf16[64,8192]{1,0:T(8,128)(2,1)}, u32[]{:S(2)}) %copy-start.1) | copy-done | bytes 1048600
  2.8 0.0 copy-start.4
  2.8 0.9 %copy-done.4 = bf16[64,1024]{1,0:T(8,128)(2,1)S(1)} copy-done((bf16[64,1024]{1,0:T(8,128)(2,1)S(1)}, bf16[64,1024]{1,0:T(8,128)(2,1)}, u32[]{:S(2)}) %copy-start.4) | copy-done | bytes 131096
  3.7 0.0 copy-start.6
  3.7 0.7 %copy-done.6 = bf16[64,128]{1,0:T(8,128)(2,1)S(1)} copy-done((bf16[64,128]{1,0:T(8,128)(2,1)S(1)}, bf16[64,128]{1,0:T(8,128)(2,1)}, u32[]{:S(2)}) %copy-start.6) | copy-done | bytes 16408
  4.4 49.0 %gather_field.1 = (bf16[512,1024]{1,0:T(8,128)(2,1)S(1)}, bf16[128,1024]{1,0:T(8,128)(2,1)S(1)}, f32[16,1024]{1,0:T(8,128)S(1)}) custom-call(bf16[16,512,128]{2,1,0:T(8,128)(2,1)S(1)} %copy-done, bf16[64,128]{1,0:T(8,128)(2,1)S(1)} %copy-done.6, bf16[64,8192]{1,0:T(8,128)(2,1)S(1)} %copy-done.1, bf16[64,1024]{1,0:T(8,128)(2,1)S(1)} %copy-done.4), custom_call_target="tpu_custom_call" | custom-call | tf_op jit(solution)/shard_map/gather_field/pallas_call | solution.py:205
  53.5 0.0 copy-start.2
  53.5 1.0 %copy-done.2 = bf16[512,1024]{1,0:T(8,128)(2,1)} copy-done((bf16[512,1024]{1,0:T(8,128)(2,1)}, bf16[512,1024]{1,0:T(8,128)(2,1)S(1)}, u32[]{:S(2)}) %copy-start.2) | copy-done | bytes 1048600
  54.4 0.0 copy-start.3
  54.4 0.7 %copy-done.3 = bf16[128,1024]{1,0:T(8,128)(2,1)} copy-done((bf16[128,1024]{1,0:T(8,128)(2,1)}, bf16[128,1024]{1,0:T(8,128)(2,1)S(1)}, u32[]{:S(2)}) %copy-start.3) | copy-done | bytes 262168
  55.1 0.0 copy-start.5
  55.1 0.6 %copy-done.5 = f32[16,1024]{1,0:T(8,128)} copy-done((f32[16,1024]{1,0:T(8,128)}, f32[16,1024]{1,0:T(8,128)S(1)}, u32[]{:S(2)}) %copy-start.5) | copy-done | bytes 65560
  55.8 5.2 %project.1 = bf16[16,512,128]{2,1,0:T(8,128)(2,1)} custom-call(bf16[512,1024]{1,0:T(8,128)(2,1)} %copy-done.2, bf16[128,1024]{1,0:T(8,128)(2,1)} %copy-done.3, f32[16,1024]{1,0:T(8,128)} %copy-done.5), custom_call_target="tpu_custom_call" | custom-call | tf_op jit(solution)/shard_map/project/pallas_call | solution.py:237
Async XLA Ops:
  0.0 1.6 %copy-start = (bf16[16,512,128]{2,1,0:T(8,128)(2,1)S(1)}, bf16[16,512,128]{2,1,0:T(8,128)(2,1)}, u32[]{:S(2)}) copy-start(bf16[16,512,128]{2,1,0:T(8,128)(2,1)} %exc_hbm.1) | copy-start | bytes 6291460
  1.6 1.2 %copy-start.1 = (bf16[64,8192]{1,0:T(8,128)(2,1)S(1)}, bf16[64,8192]{1,0:T(8,128)(2,1)}, u32[]{:S(2)}) copy-start(bf16[64,8192]{1,0:T(8,128)(2,1)} %cond_hbm.1) | copy-start | bytes 3145732
  2.8 0.9 %copy-start.4 = (bf16[64,1024]{1,0:T(8,128)(2,1)S(1)}, bf16[64,1024]{1,0:T(8,128)(2,1)}, u32[]{:S(2)}) copy-start(bf16[64,1024]{1,0:T(8,128)(2,1)} %scr_ref.1) | copy-start | bytes 393220
  3.7 0.7 %copy-start.6 = (bf16[64,128]{1,0:T(8,128)(2,1)S(1)}, bf16[64,128]{1,0:T(8,128)(2,1)}, u32[]{:S(2)}) copy-start(bf16[64,128]{1,0:T(8,128)(2,1)} %val_ref.1) | copy-start | bytes 49156
  53.5 1.0 %copy-start.2 = (bf16[512,1024]{1,0:T(8,128)(2,1)}, bf16[512,1024]{1,0:T(8,128)(2,1)S(1)}, u32[]{:S(2)}) copy-start(bf16[512,1024]{1,0:T(8,128)(2,1)S(1)} %get-tuple-element.8.condt_ref) | copy-start | bytes 3145732
  54.4 0.7 %copy-start.3 = (bf16[128,1024]{1,0:T(8,128)(2,1)}, bf16[128,1024]{1,0:T(8,128)(2,1)S(1)}, u32[]{:S(2)}) copy-start(bf16[128,1024]{1,0:T(8,128)(2,1)S(1)} %get-tuple-element.9.valt_ref) | copy-start | bytes 786436
  55.1 0.6 %copy-start.5 = (f32[16,1024]{1,0:T(8,128)}, f32[16,1024]{1,0:T(8,128)S(1)}, u32[]{:S(2)}) copy-start(f32[16,1024]{1,0:T(8,128)S(1)} %get-tuple-element.10.field_ref) | copy-start | bytes 196612

commit v2 on v1

--- a/solution.py
+++ b/solution.py
@@ -21,12 +21,32 @@
     return total
 
 
+def send_order(n, q):
+    far = list(range(n - 1, n // 2 - 1, -1))
+    near = [1] + [k for k in range(n // 2 - 1, 1, -1) if k // 2 != q // 4]
+    near[3:3] = [k for k in range(n // 2 - 1, 1, -1) if k // 2 == q // 4]
+    order = []
+    while far or near:
+        order += far[:2] + near[:3]
+        far, near = far[2:], near[3:]
+    return order
+
+
+def work_order(n, q):
+    seen, order = {0}, [0]
+    for k in send_order(n, q):
+        seen.add(k)
+        if seen >= {k, k ^ 1} and k // 2 not in order:
+            order.append(k // 2)
+    return order
+
+
 def gather_kernel(
     n, planes,
     exc_hbm, val_ref, cond_hbm, scr_ref,
-    condt_ref, valt_ref, field_ref,
-    exc, exct, cond_all, val_all, scr_chip, part, red, dens, dens_all, fld, fld_all,
-    exc_sem, own_sem,
+    condt_hbm, valt_hbm, field_hbm,
+    condt_ref, valt_ref, field_ref, exc, exct, cond_all, val_all, scr_chip, part, red, dens, dens_all, fld, fld_all,
+    exc_sem, own_sem, out_sem, field_sem,
     cond_send, cond_recv, scr_send, scr_recv, va_send, va_recv, vb_send, vb_recv,
     part_send, part_recv, dens_send, dens_recv, fld_send, fld_recv,
 ):
@@ -68,7 +88,7 @@
         copy = remote(val_ref, val_all.at[my_q, my_z], va_send.at[k], va_recv.at[my_z], to)
         copy.start()
         sent.append(copy)
-    for k in range(n - 1, 0, -1):
+    for k in send_order(n, q):
         to = flip(me, k, bits)
         copy = remote(
             cond_hbm.at[:, pl.ds(pl.multiple_of(to * cl, cl), cl)], cond_all.at[me],
@@ -101,7 +121,10 @@
         other = flip(my_q, k, qbits)
         pltpu.make_async_copy(val_all.at[other], val_all.at[other], vb_recv.at[other]).wait()
 
-    def group(k, carry):
+    def group(step, carry):
+        k = 0
+        for at, value in enumerate(work_order(n, q)):
+            k = k + jnp.where(step == at, value, 0)
         p = flip(chip, k, bits - 1)
         z, y = p // (q // 2), p % (q // 2)
         lanes = pl.ds(pl.multiple_of(p * 2 * rows, 2 * rows), 2 * rows)
@@ -132,6 +155,8 @@
                 ).start()
 
         condt_ref[:, lanes] = block.T
+        pltpu.make_async_copy(condt_ref.at[:, lanes], condt_hbm.at[:, lanes], out_sem.at[k, 0]).start()
+        pltpu.make_async_copy(valt_ref.at[:, lanes], valt_hbm.at[:, lanes], out_sem.at[k, 1]).start()
         return carry
 
     lax.fori_loop(0, chips, group, 0)
@@ -169,6 +194,14 @@
         for h in range(2):
             field_ref[h * half:(h + 1) * half, p * 2 * rows:(p + 1) * 2 * rows] = fld_all[2 * p + h].astype(jnp.float32)
 
+    field_copy = pltpu.make_async_copy(field_ref, field_hbm, field_sem)
+    field_copy.start()
+    for k in range(chips):
+        lanes = pl.ds(pl.multiple_of(flip(chip, k, bits - 1) * 2 * rows, 2 * rows), 2 * rows)
+        pltpu.make_async_copy(condt_ref.at[:, lanes], condt_hbm.at[:, lanes], out_sem.at[k, 0]).wait()
+        pltpu.make_async_copy(valt_ref.at[:, lanes], valt_hbm.at[:, lanes], out_sem.at[k, 1]).wait()
+    field_copy.wait()
+
     for copy in sent:
         copy.wait_send()
     remote(
@@ -180,17 +213,33 @@
             remote(part.at[k, h], red.at[me], part_send.at[k, h], part_recv.at[me], 2 * p + h).wait_send()
 
 
-def project_kernel(per, condt_ref, valt_ref, field_ref, out_ref):
-    step = pl.program_id(0)
+def project_kernel(condt_hbm, valt_hbm, field_hbm, out_hbm, condt_ref, valt_ref, field_ref, held, in_sem, out_sem):
+    loads = [
+        pltpu.make_async_copy(src, dst, in_sem.at[at])
+        for at, (src, dst) in enumerate(((valt_hbm, valt_ref), (field_hbm, field_ref), (condt_hbm, condt_ref)))
+    ]
+    for load in loads:
+        load.start()
+    loads[0].wait()
+    loads[1].wait()
     v = valt_ref.shape[0]
+    batch = field_ref.shape[0]
     valt = valt_ref[...].astype(jnp.float32)
-    for j in range(0, per, 2):
+    copies = []
+    for b in range(0, batch, 2):
         weights = jnp.concatenate(
-            [(valt * field_ref[pl.ds(step * per + j + i, 1), :]).astype(jnp.bfloat16) for i in range(2)], axis=0
+            [(valt * field_ref[b + i:b + i + 1, :]).astype(jnp.bfloat16) for i in range(2)], axis=0
         )
+        if b == 0:
+            loads[2].wait()
         summed = lax.dot_general(condt_ref[...], weights, NT, preferred_element_type=jnp.float32)
         for i in range(2):
-            out_ref[j + i] = summed[:, i * v:(i + 1) * v].astype(jnp.bfloat16)
+            held[b + i] = summed[:, i * v:(i + 1) * v].astype(jnp.bfloat16)
+        copy = pltpu.make_async_copy(held.at[pl.ds(b, 2)], out_hbm.at[pl.ds(b, 2)], out_sem.at[b // 2])
+        copy.start()
+        copies.append(copy)
+    for copy in copies:
+        copy.wait()
 
 
 def fast_body(n, excitations, valence_orb, conduction_orb, screened):
@@ -199,8 +248,7 @@
     planes = 4 if n % 8 == 0 else 2
     q, chips, half = n // planes, n // 2, batch // 2
     bf, f32 = jnp.bfloat16, jnp.float32
-    any_ = pl.BlockSpec(memory_space=pl.ANY)
-    vmem = pl.BlockSpec(memory_space=pltpu.VMEM)
+    hbm = pl.BlockSpec(memory_space=pltpu.HBM)
     dma = pltpu.SemaphoreType.DMA
     condt, valt, field = pl.pallas_call(
         functools.partial(gather_kernel, n, planes),
@@ -209,9 +257,12 @@
             jax.ShapeDtypeStruct((v, points), bf),
             jax.ShapeDtypeStruct((batch, points), f32),
         ),
-        in_specs=[any_, vmem, any_, vmem],
-        out_specs=(vmem, vmem, vmem),
+        in_specs=[hbm, hbm, hbm, hbm],
+        out_specs=(hbm, hbm, hbm),
         scratch_shapes=[
+            pltpu.VMEM((cl, points), bf),
+            pltpu.VMEM((v, points), bf),
+            pltpu.VMEM((batch, points), f32),
             pltpu.VMEM((batch, cl, v), bf),
             pltpu.VMEM((batch * v, cl), bf),
             pltpu.VMEM((n, rows, cl), bf),
@@ -223,27 +274,24 @@
             pltpu.VMEM((chips, half, 2 * rows), bf),
             pltpu.VMEM((half, 2 * rows), bf),
             pltpu.VMEM((n, half, 2 * rows), bf),
-            dma, dma((2,)),
+            dma, dma((2,)), dma((chips, 2)), dma,
             dma((n,)), dma((n,)), dma, dma, dma((planes,)), dma((planes,)), dma((q,)), dma((q,)),
             dma((chips, 2)), dma((n,)), dma((chips,)), dma((chips,)), dma((n,)), dma((n,)),
         ],
         compiler_params=pltpu.CompilerParams(
-            collective_id=0, has_side_effects=True, vmem_limit_bytes=40 * 1024 * 1024
+            collective_id=0, has_side_effects=True, vmem_limit_bytes=63 * 1024 * 1024
         ),
         name="gather_field",
     )(excitations, valence_orb, conduction_orb, screened)
-    per = 4
-    whole = lambda i: (0, 0)
     return pl.pallas_call(
-        functools.partial(project_kernel, per),
-        grid=(batch // per,),
+        project_kernel,
         out_shape=jax.ShapeDtypeStruct((batch, cl, v), bf),
-        in_specs=[
-            pl.BlockSpec((cl, points), whole),
-            pl.BlockSpec((v, points), whole),
-            pl.BlockSpec((batch, points), whole),
-        ],
-        out_specs=pl.BlockSpec((per, cl, v), lambda i: (i, 0, 0)),
+        in_specs=[hbm, hbm, hbm],
+        out_specs=hbm,
+        scratch_shapes=[
+            pltpu.VMEM((cl, points), bf), pltpu.VMEM((v, points), bf), pltpu.VMEM((batch, points), f32),
+            pltpu.VMEM((batch, cl, v), bf), dma((3,)), dma((batch // 2,))],
+        compiler_params=pltpu.CompilerParams(vmem_limit_bytes=63 * 1024 * 1024),
         name="project",
     )(condt, valt, field)
 

time: 61.2 us -> 51.8 us (0.85)
  local copies, waits for them, and re-layouts: 6.71 us -> 0 us
  Pallas kernels: 54.2 us -> 51.6 us
    unnamed x14 -> x0, local copies, waits for them, and re-layouts: 6.71 us -> none
    pallas_call x1, Pallas kernels: 49 us -> 46.9 us  [fast_body(): pl.pallas_call(functools.partial(gather_kernel, n, planes), out_shape=(ja...]
where the time goes in v2:
time: 51.8 us; the launch traced here: 51.6 us
  Pallas kernels  51.6 us (100%)
    pallas_call x1, Pallas kernels, fast_body(): pl.pallas_call(functools.partial(gather_kernel, n, planes), out_shape=(ja...  46.9 us
    pallas_call x1, Pallas kernels, fast_body(): pl.pallas_call(project_kernel, out_shape=jax.ShapeDtypeStruct((batch, cl,...  4.69 us

profile of v2, /device:TPU:0, one launch (start us, length us, event | category | flops | bytes accessed | tf_op | source)
XLA Modules:
  0.0 51.6 jit_solution(12948578795891083045)
XLA Ops:
  0.0 46.9 %gather_field.1 = (bf16[512,1024]{1,0:T(8,128)(2,1)}, bf16[128,1024]{1,0:T(8,128)(2,1)}, f32[16,1024]{1,0:T(8,128)}) custom-call(bf16[16,512,128]{2,1,0:T(8,128)(2,1)} %exc_hbm.1, bf16[64,128]{1,0:T(8,128)(2,1)} %val_ref.1, bf16[64,8192]{1,0:T(8,128)(2,1)} %cond_hbm.1, bf16[64,1024]{1,0:T(8,128)(2,1)} %scr_ref.1), custom_call_target="tpu_custom_call" | custom-call | tf_op jit(solution)/shard_map/gather_field/pallas_call | solution.py:253
  46.9 4.7 %project.1 = bf16[16,512,128]{2,1,0:T(8,128)(2,1)} custom-call(bf16[512,1024]{1,0:T(8,128)(2,1)} %get-tuple-element.8.condt_hbm, bf16[128,1024]{1,0:T(8,128)(2,1)} %get-tuple-element.9.valt_hbm, f32[16,1024]{1,0:T(8,128)} %get-tuple-element.10.field_hbm), custom_call_target="tpu_custom_call" | custom-call | tf_op jit(solution)/shard_map/project/pallas_call | solution.py:286

commit v3 on v2

--- a/solution.py
+++ b/solution.py
@@ -200,8 +200,6 @@
         lanes = pl.ds(pl.multiple_of(flip(chip, k, bits - 1) * 2 * rows, 2 * rows), 2 * rows)
         pltpu.make_async_copy(condt_ref.at[:, lanes], condt_hbm.at[:, lanes], out_sem.at[k, 0]).wait()
         pltpu.make_async_copy(valt_ref.at[:, lanes], valt_hbm.at[:, lanes], out_sem.at[k, 1]).wait()
-    field_copy.wait()
-
     for copy in sent:
         copy.wait_send()
     remote(
@@ -211,6 +209,7 @@
         p = flip(chip, k, bits - 1)
         for h in range(2):
             remote(part.at[k, h], red.at[me], part_send.at[k, h], part_recv.at[me], 2 * p + h).wait_send()
+    field_copy.wait()
 
 
 def project_kernel(condt_hbm, valt_hbm, field_hbm, out_hbm, condt_ref, valt_ref, field_ref, held, in_sem, out_sem):
@@ -224,18 +223,18 @@
     loads[1].wait()
     v = valt_ref.shape[0]
     batch = field_ref.shape[0]
-    valt = valt_ref[...].astype(jnp.float32)
+    valt = valt_ref[...]
     copies = []
-    for b in range(0, batch, 2):
+    for b in range(0, batch, 4):
         weights = jnp.concatenate(
-            [(valt * field_ref[b + i:b + i + 1, :]).astype(jnp.bfloat16) for i in range(2)], axis=0
+            [valt * field_ref[b + i:b + i + 1, :].astype(jnp.bfloat16) for i in range(4)], axis=0
         )
         if b == 0:
             loads[2].wait()
         summed = lax.dot_general(condt_ref[...], weights, NT, preferred_element_type=jnp.float32)
-        for i in range(2):
+        for i in range(4):
             held[b + i] = summed[:, i * v:(i + 1) * v].astype(jnp.bfloat16)
-        copy = pltpu.make_async_copy(held.at[pl.ds(b, 2)], out_hbm.at[pl.ds(b, 2)], out_sem.at[b // 2])
+        copy = pltpu.make_async_copy(held.at[pl.ds(b, 4)], out_hbm.at[pl.ds(b, 4)], out_sem.at[b // 4])
         copy.start()
         copies.append(copy)
     for copy in copies:

time: 51.8 us -> 51.6 us (level)
  no operation moved by 1% of the time
where the time goes in v3:
time: 51.6 us; the launch traced here: 51.5 us
  Pallas kernels  51.4 us (100%)
    pallas_call x1, Pallas kernels, fast_body(): pl.pallas_call(functools.partial(gather_kernel, n, planes), out_shape=(ja...  46.8 us
    pallas_call x1, Pallas kernels, fast_body(): pl.pallas_call(project_kernel, out_shape=jax.ShapeDtypeStruct((batch, cl,...  4.61 us

profile of v3, /device:TPU:0, one launch (start us, length us, event | category | flops | bytes accessed | tf_op | source)
XLA Modules:
  0.0 51.5 jit_solution(5602491273913235114)
XLA Ops:
  0.0 46.8 %gather_field.1 = (bf16[512,1024]{1,0:T(8,128)(2,1)}, bf16[128,1024]{1,0:T(8,128)(2,1)}, f32[16,1024]{1,0:T(8,128)}) custom-call(bf16[16,512,128]{2,1,0:T(8,128)(2,1)} %exc_hbm.1, bf16[64,128]{1,0:T(8,128)(2,1)} %val_ref.1, bf16[64,8192]{1,0:T(8,128)(2,1)} %cond_hbm.1, bf16[64,1024]{1,0:T(8,128)(2,1)} %scr_ref.1), custom_call_target="tpu_custom_call" | custom-call | tf_op jit(solution)/shard_map/gather_field/pallas_call | solution.py:252
  46.8 4.6 %project.1 = bf16[16,512,128]{2,1,0:T(8,128)(2,1)} custom-call(bf16[512,1024]{1,0:T(8,128)(2,1)} %get-tuple-element.8.condt_hbm, bf16[128,1024]{1,0:T(8,128)(2,1)} %get-tuple-element.9.valt_hbm, f32[16,1024]{1,0:T(8,128)} %get-tuple-element.10.field_hbm), custom_call_target="tpu_custom_call" | custom-call | tf_op jit(solution)/shard_map/project/pallas_call | solution.py:285
